TPU v7x, 128 devices: a whole 4x4x4 slice. The times are simulated.
128 devices in a mesh: grp: 8 (over x, y_lo), blk: 16 (over z, y_hi, core).
Axes of the slice: x: 4, y: 4 (y_hi: 2, y_lo: 2; y = y_hi * 2 + y_lo), z: 4, core: 2. Of those that a mesh axis runs over, the one named last changes fastest.
Arguments:
- source_emb: bfloat16 [24576, 768], P('blk'), may hold values from -32 to 32
- target_emb: bfloat16 [24576, 768], P(('grp', 'blk')), may hold values from -16 to 16
- hard_pool: bfloat16 [24576, 768], P(('grp', 'blk')), may hold values from -16 to 16
- hard_index: int32 [24576], P('blk'), may hold values from 0 to 24575, as said below
- language: int32 [24576], P('blk'), may hold values from 0 to 108
- margin: float32 [109], replicated, may hold values from 0.5 to 3
Outputs:
- row_loss: float32 [24576], P('blk')
- source_grad: float32 [24576, 768], P('blk')
- target_grad: float32 [24576, 768], P(('grp', 'blk'))
- pool_grad: float32 [24576, 768], P(('grp', 'blk'))
Inputs may be any that keep to these rules, and one draw needn't show every extreme that they name: `hard_index`: each entry is a row of hard_pool; an entry's owner is its value // 192. Within each aligned block of 192 entries no owner is named more than 3 times, and one owner, the same for all blocks, is named exactly 3 times in every block.
All inputs are finite; a program needn't handle non-finite values.
Results may differ from a plain program's by a relative error of at most 0.0025.
Values may be sent and summed in bfloat16 or wider, within the bound.
No kernel may reach another device: no remote copies, remote signals or barrier semaphores. Data moves between devices by JAX's collectives and lax.ppermute only.
A program may use at most 64 MiB of HBM per device.

v0:
```python
import jax
import jax.numpy as jnp
from jax import lax
from jax.sharding import PartitionSpec as P

neg_fill = -1e30


def shifted(block, axis, distance):
    devices = range(lax.axis_size(axis))
    route = [((i - distance) % len(devices), i) for i in devices]
    return lax.ppermute(block, axis, route)


def merged(value, axis, join):
    pieces = jax.tree.map(lambda part: lax.all_gather(part, axis), value)
    head = jax.tree.map(lambda part: part[0], pieces)
    tail = jax.tree.map(lambda part: part[1:], pieces)
    so_far, _ = lax.scan(lambda so_far, piece: (join(so_far, piece), None), head, tail)
    return so_far


def combine(earlier, later):
    row_top = jnp.maximum(earlier[0], later[0])
    row_total = earlier[1] * jnp.exp(earlier[0] - row_top) + later[1] * jnp.exp(later[0] - row_top)
    return (row_top, row_total, earlier[2] + later[2])


def serve_rows(hard_pool, wanted):
    is_valid = wanted >= 0
    picked = jnp.take(hard_pool, jnp.maximum(wanted, 0), axis=0)
    return jnp.where(is_valid[..., None], picked, jnp.zeros_like(picked))


def shards(source_emb, target_emb, hard_pool, hard_index, language, margin):
    row_count = source_emb.shape[0]
    width = source_emb.shape[1]
    tgt_rows = target_emb.shape[0]
    blk_count = lax.axis_size("blk")
    grp_count = lax.axis_size("grp")
    owner_count = blk_count * grp_count
    slot_cap = max(2, (2 * tgt_rows + owner_count - 1) // owner_count)
    blk_index = lax.axis_index("blk")
    grp_index = lax.axis_index("grp")
    row_ids = blk_index * row_count + jnp.arange(row_count, dtype=jnp.int32)
    lang_match = language[:, None] == jnp.arange(margin.shape[0], dtype=jnp.int32)[None, :]
    margin_row = jnp.sum(jnp.where(lang_match, margin[None, :], 0.0), axis=1)
    column = jnp.arange(tgt_rows, dtype=jnp.int32)

    def global_cols(step_index):
        col_back = (
            grp_index * blk_count + (blk_index - step_index) % blk_count
        ) * tgt_rows + column
        return col_back

    def adjusted_scores(tgt_block, step_index):
        scores = jnp.einsum("rd,td->rt", source_emb, tgt_block, preferred_element_type=jnp.float32)
        positive = row_ids[:, None] == global_cols(step_index)[None, :]
        return (scores - jnp.where(positive, margin_row[:, None], 0.0), positive)

    own_start = grp_index * tgt_rows
    own_index = lax.dynamic_slice_in_dim(hard_index, own_start, tgt_rows, 0)
    own_source = lax.dynamic_slice_in_dim(source_emb, own_start, tgt_rows, 0)
    owner_index = own_index // tgt_rows
    pool_row = own_index % tgt_rows
    position = jnp.arange(tgt_rows, dtype=jnp.int32)
    earlier_same = (owner_index[:, None] == owner_index[None, :]) & (
        position[None, :] < position[:, None]
    )
    slot_index = jnp.sum(earlier_same.astype(jnp.int32), axis=1)
    requests = (
        jnp.full((owner_count, slot_cap), -1, jnp.int32).at[owner_index, slot_index].set(pool_row)
    )
    wanted = lax.all_to_all(requests, ("grp", "blk"), split_axis=0, concat_axis=0, tiled=True)
    served = serve_rows(hard_pool, wanted)
    fetched = lax.all_to_all(served, ("grp", "blk"), split_axis=0, concat_axis=0, tiled=True)
    hard_rows = fetched[owner_index, slot_index]
    hard_score = jnp.einsum("rd,rd->r", own_source, hard_rows, preferred_element_type=jnp.float32)
    top_start = jnp.full((row_count,), neg_fill, jnp.float32)
    top_start = lax.dynamic_update_slice_in_dim(top_start, hard_score, own_start, 0)
    total_start = jnp.zeros((row_count,), jnp.float32)
    total_start = lax.dynamic_update_slice_in_dim(
        total_start, jnp.ones((tgt_rows,), jnp.float32), own_start, 0
    )
    positive_start = jnp.zeros((row_count,), jnp.float32)

    def absorb(partials, tgt_block, step_index):
        row_top, row_total, positive_sum = partials
        adjusted, positive = adjusted_scores(tgt_block, step_index)
        new_top = jnp.maximum(row_top, jnp.max(adjusted, axis=1))
        row_total = row_total * jnp.exp(row_top - new_top) + jnp.sum(
            jnp.exp(adjusted - new_top[:, None]), axis=1
        )
        positive_sum = positive_sum + jnp.sum(jnp.where(positive, adjusted, 0.0), axis=1)
        return (new_top, row_total, positive_sum)

    def forward(step_index, loop_state):
        tgt_block, partials, stored = loop_state
        partials = absorb(partials, tgt_block, step_index)
        stored = lax.dynamic_update_index_in_dim(stored, tgt_block, step_index, 0)
        tgt_block = shifted(tgt_block, "blk", 1)
        return (tgt_block, partials, stored)

    stored = jnp.zeros((blk_count, tgt_rows, width), target_emb.dtype)
    start_state = (target_emb, (top_start, total_start, positive_start), stored)
    tgt_block, partials, stored = lax.fori_loop(0, blk_count - 1, forward, start_state)
    last_step = blk_count - 1
    partials = absorb(partials, tgt_block, last_step)
    stored = lax.dynamic_update_index_in_dim(stored, tgt_block, last_step, 0)
    row_top, row_total, positive_sum = merged(partials, "grp", combine)
    log_total = row_top + jnp.log(row_total)
    row_loss = log_total - positive_sum

    def backward(step_index, loop_state):
        grad_block, source_acc = loop_state
        tgt_block = lax.dynamic_index_in_dim(stored, step_index, 0, keepdims=False)
        adjusted, positive = adjusted_scores(tgt_block, step_index)
        prob_tile = (jnp.exp(adjusted - log_total[:, None]) - positive.astype(jnp.float32)).astype(
            jnp.bfloat16
        )
        source_acc = source_acc + jnp.einsum(
            "rt,td->rd", prob_tile, tgt_block, preferred_element_type=jnp.float32
        )
        grad_block = grad_block + jnp.einsum(
            "rt,rd->td", prob_tile, source_emb, preferred_element_type=jnp.float32
        )
        grad_block = shifted(grad_block, "blk", 1)
        return (grad_block, source_acc)

    back_start = (
        jnp.zeros((tgt_rows, width), jnp.float32),
        jnp.zeros((row_count, width), jnp.float32),
    )
    target_grad, source_acc = lax.fori_loop(0, blk_count, backward, back_start)
    own_total = lax.dynamic_slice_in_dim(log_total, own_start, tgt_rows, 0)
    hard_prob = jnp.exp(hard_score - own_total)
    own_acc = lax.dynamic_slice_in_dim(source_acc, own_start, tgt_rows, 0)
    own_acc = own_acc + hard_prob[:, None] * hard_rows.astype(jnp.float32)
    source_acc = lax.dynamic_update_slice_in_dim(source_acc, own_acc, own_start, 0)
    source_grad = lax.psum(source_acc, "grp")
    contribution = hard_prob[:, None] * own_source.astype(jnp.float32)
    outgoing = (
        jnp.zeros((owner_count, slot_cap, width), jnp.float32)
        .at[owner_index, slot_index]
        .set(contribution)
    )
    incoming = lax.all_to_all(outgoing, ("grp", "blk"), split_axis=0, concat_axis=0, tiled=True)
    is_valid = wanted >= 0
    kept = jnp.where(is_valid[..., None], incoming, 0.0).reshape(owner_count * slot_cap, width)
    pool_grad = (
        jnp.zeros((tgt_rows, width), jnp.float32).at[jnp.maximum(wanted, 0).reshape(-1)].add(kept)
    )
    return (row_loss, source_grad, target_grad, pool_grad)


def solution(mesh):
    in_specs = (
        P("blk", None),
        P(("grp", "blk"), None),
        P(("grp", "blk"), None),
        P("blk"),
        P("blk"),
        P(),
    )
    out_specs = (P("blk"), P("blk", None), P(("grp", "blk"), None), P(("grp", "blk"), None))
    return jax.shard_map(shards, mesh=mesh, in_specs=in_specs, out_specs=out_specs, check_vma=False)
```

profile of v0, /device:TPU:0, one launch (start us, length us, event | category | flops | bytes accessed | tf_op | source)
XLA Modules:
  0.0 840.6 jit_solution(6515068497851524991)
XLA Ops:
  8.2 9.3 %scatter_fusion = s32[128,3]{0,1:T(4,128)S(1)} fusion(s32[128,3]{0,1:T(4,128)S(1)} %broadcast_in_dim.189, s32[192]{0:T(256)S(1)} %bitcast.74, s32[192]{0:T(256)S(1)} %get-tuple-element.767), kind=kCustom, calls=%fused_computation.2 | custom fusion | bytes 3840 | tf_op jit(solution)/shard_map/scatter | solution.py:72
  17.6 20.4 %all_to_all.19 = s32[128,1,3]{2,1,0:T(1,128)S(1)} all-to-all(s32[128,1,3]{2,1,0:T(1,128)S(1)} %copy.41), channel_id=1, replica_groups=mesh['grp'=8,'blk'=16] {'grp','blk'}, dimensions={0} | all-to-all | bytes 3072 | tf_op jit(solution)/shard_map/all_to_all | solution.py:74
  51.8 12.4 %all-to-all-done.1 = bf16[128,3,768]{2,1,0:T(4,128)(2,1)S(1)} async-done(((bf16[128,3,768]{2,1,0:T(4,128)(2,1)}), bf16[128,3,768]{2,1,0:T(4,128)(2,1)S(1)}, u32[]{:S(2)}, u32[]{:S(2)}) %all-to-all-start.1) | async-done | bytes 589856 | tf_op jit(solution)/shard_map/all_to_all | solution.py:76
  72.1 147.8 %while.57 = (s32[]{:T(128)}, bf16[192,768]{1,0:T(8,128)(2,1)S(1)}, f32[1536]{0:T(1024)}, f32[1536]{0:T(1024)}, f32[1536]{0:T(1024)}, /*index=5*/bf16[16,192,768]...) while((s32[]{:T(128)}, bf16[192,768]{1,0:T(8,128)(2,1)S(1)}, ...), condition=%wide.region_7.8_spmd.clone, body=%wide.region_3.7_spmd.clone.sunk | while | flops 455645376 | bytes 7504492 | solution.py:106
  222.4 28.3 %all-gather.3 = f32[8,1,1536]{2,1,0:T(1,128)S(1)} all-gather(f32[1,1,1536]{2,1,0:T(1,128)S(1)} %reshape.152), channel_id=2, replica_groups=mesh['grp'=8,'blk'=16] {'grp'}, dimensions={0}, use_global_device_ids=true | all-gather | bytes 55296 | tf_op jit(solution)/shard_map/all_gather | solution.py:16
  251.8 28.3 %all-gather.4 = f32[8,1,1536]{2,1,0:T(1,128)S(1)} all-gather(f32[1,1,1536]{2,1,0:T(1,128)S(1)} %reshape.154), channel_id=3, replica_groups=mesh['grp'=8,'blk'=16] {'grp'}, dimensions={0}, use_global_device_ids=true | all-gather | bytes 55296 | tf_op jit(solution)/shard_map/all_gather | solution.py:16
  280.9 28.5 %all-gather.5 = f32[8,1,1536]{2,1,0:T(1,128)S(1)} all-gather(f32[1,1,1536]{2,1,0:T(1,128)S(1)} %reshape.156), channel_id=4, replica_groups=mesh['grp'=8,'blk'=16] {'grp'}, dimensions={0}, use_global_device_ids=true | all-gather | bytes 55296 | tf_op jit(solution)/shard_map/all_gather | solution.py:16
  310.0 6.5 while.56
  319.4 292.8 %while.58 = (s32[]{:T(128)}, f32[192,768]{1,0:T(8,128)}, f32[1536,768]{1,0:T(8,128)}, bf16[16,192,768]{2,1,0:T(8,128)(2,1)}, bf16[1536,768]{1,0:T(8,128)(2,1)S(1...) while((s32[]{:T(128)}, f32[192,768]{1,0:T(8,128)}, ...), condition=%wide.region_14.15_spmd.clone, body=%wide.region_13.14_spmd.clone.sunk | while | flops 1363527424 | bytes 20133792 | solution.py:134
  328.4 9.3 %collective-permute-done.1 = f32[192,768]{1,0:T(8,128)} collective-permute-done((f32[192,768]{1,0:T(8,128)}, f32[192,768]{1,0:T(8,128)}, u32[]{:S(2)}, u32[]{:S(2)}) %collective-permute-start.1) | collective-permute-done | bytes 589856 | tf_op jit(solution)/shard_map/while/body/eval_jaxpr/ppermute | solution.py:12
  342.7 5.4 select_add_fusion.5
  348.1 7.8 collective-permute-done.1
  366.4 7.8 collective-permute-done.1
  379.3 5.4 select_add_fusion.5
  384.7 7.8 collective-permute-done.1
  397.6 5.4 select_add_fusion.5
  403.0 7.8 collective-permute-done.1
  421.3 7.8 collective-permute-done.1
  434.2 5.4 select_add_fusion.5
  439.6 7.8 collective-permute-done.1
  457.9 7.8 collective-permute-done.1
  476.3 7.8 collective-permute-done.1
  494.5 7.8 collective-permute-done.1
  512.9 7.8 collective-permute-done.1
  531.2 7.8 collective-permute-done.1
  549.5 7.8 collective-permute-done.1
  567.8 7.8 collective-permute-done.1
  586.1 7.8 collective-permute-done.1
  604.4 7.8 collective-permute-done.1
  614.3 11.1 %scatter_fusion.1 = f32[128,3,768]{2,0,1:T(8,128)S(1)} fusion(f32[128,3,768]{2,0,1:T(8,128)S(1)} %broadcast_in_dim.203, s32[192]{0:T(256)S(1)} %bitcast.75, f32[192,768]{1,0:T(8,128)S(1)} %get-tuple-element.770), kind=kCustom, calls=%fused_computation.3 | custom fusion | bytes 1771008 | tf_op jit(solution)/shard_map/scatter | solution.py:145
  632.1 30.3 %all-to-all-done.2 = f32[128,3,768]{2,1,0:T(4,128)S(1)} async-done(((f32[128,3,768]{2,1,0:T(4,128)}), f32[128,3,768]{2,1,0:T(4,128)S(1)}, u32[]{:S(2)}, u32[]{:S(2)}) %all-to-all-start.2) | async-done | bytes 1179680 | tf_op jit(solution)/shard_map/all_to_all | solution.py:147
  668.2 158.8 %all-reduce.2.cloned.1.call-done = f32[1536,768]{1,0:T(8,128)} async-done(((f32[1536,768]{1,0:T(8,128)}), f32[1536,768]{1,0:T(8,128)}) %all-reduce.2.cloned.1.call-update) | async-done | bytes 4718608 | tf_op jit(solution)/shard_map/psum | solution.py:140
  (434 shorter events, 349.2 us)
Async XLA Ops:
  43.2 21.0 %all-to-all-start.1 = ((bf16[128,3,768]{2,1,0:T(4,128)(2,1)}), bf16[128,3,768]{2,1,0:T(4,128)(2,1)S(1)}, u32[]{:S(2)}, u32[]{:S(2)}) async-start(bf16[128,3,768]{2,1,0:T(4,128)(2,1)} %copy.46), calls=%async_computation.1 | async-start | bytes 1572864 | tf_op jit(solution)/shard_map/all_to_all | solution.py:76
  47.8 779.2 %all-reduce.2.cloned.1.call-start = ((), (), s32[]{:S(2)}) async-start(), calls=%async_computation.3 | async-start | bytes 9437184 | tf_op jit(solution)/shard_map/psum | solution.py:140
  72.1 9.8 %collective-permute-start = (bf16[192,768]{1,0:T(8,128)(2,1)S(1)}, bf16[192,768]{1,0:T(8,128)(2,1)S(1)}, u32[]{:S(2)}, u32[]{:S(2)}) collective-permute-start(bf16[192,768]{1,0:T(8,128)(2,1)S(1)} %copy.84), channel_id=1, source_target_pairs={{15,0},{0,1},{1,2},{2,3},{3,4},{4,5},{5,6},{6,7},{7,8},{8,9},{9,10... | collective-permute-start | bytes 884744 | tf_op jit(solution)/shard_map/while/body/eval_jaxpr/ppermute | solution.py:12
  82.0 9.8 %collective-permute-start = (bf16[192,768]{1,0:T(8,128)(2,1)S(1)}, bf16[192,768]{1,0:T(8,128)(2,1)S(1)}, u32[]{:S(2)}, u32[]{:S(2)}) collective-permute-start(bf16[192,768]{1,0:T(8,128)(2,1)S(1)} %copy.84), channel_id=1, source_target_pairs={{15,0},{0,1},{1,2},{2,3},{3,4},{4,5},{5,6},{6,7},{7,8},{8,9},{9,10... | collective-permute-start | bytes 884744 | tf_op jit(solution)/shard_map/while/body/eval_jaxpr/ppermute | solution.py:12
  91.9 9.8 %collective-permute-start = (bf16[192,768]{1,0:T(8,128)(2,1)S(1)}, bf16[192,768]{1,0:T(8,128)(2,1)S(1)}, u32[]{:S(2)}, u32[]{:S(2)}) collective-permute-start(bf16[192,768]{1,0:T(8,128)(2,1)S(1)} %copy.84), channel_id=1, source_target_pairs={{15,0},{0,1},{1,2},{2,3},{3,4},{4,5},{5,6},{6,7},{7,8},{8,9},{9,10... | collective-permute-start | bytes 884744 | tf_op jit(solution)/shard_map/while/body/eval_jaxpr/ppermute | solution.py:12
  101.7 9.8 %collective-permute-start = (bf16[192,768]{1,0:T(8,128)(2,1)S(1)}, bf16[192,768]{1,0:T(8,128)(2,1)S(1)}, u32[]{:S(2)}, u32[]{:S(2)}) collective-permute-start(bf16[192,768]{1,0:T(8,128)(2,1)S(1)} %copy.84), channel_id=1, source_target_pairs={{15,0},{0,1},{1,2},{2,3},{3,4},{4,5},{5,6},{6,7},{7,8},{8,9},{9,10... | collective-permute-start | bytes 884744 | tf_op jit(solution)/shard_map/while/body/eval_jaxpr/ppermute | solution.py:12
  111.6 9.8 %collective-permute-start = (bf16[192,768]{1,0:T(8,128)(2,1)S(1)}, bf16[192,768]{1,0:T(8,128)(2,1)S(1)}, u32[]{:S(2)}, u32[]{:S(2)}) collective-permute-start(bf16[192,768]{1,0:T(8,128)(2,1)S(1)} %copy.84), channel_id=1, source_target_pairs={{15,0},{0,1},{1,2},{2,3},{3,4},{4,5},{5,6},{6,7},{7,8},{8,9},{9,10... | collective-permute-start | bytes 884744 | tf_op jit(solution)/shard_map/while/body/eval_jaxpr/ppermute | solution.py:12
  121.4 9.8 %collective-permute-start = (bf16[192,768]{1,0:T(8,128)(2,1)S(1)}, bf16[192,768]{1,0:T(8,128)(2,1)S(1)}, u32[]{:S(2)}, u32[]{:S(2)}) collective-permute-start(bf16[192,768]{1,0:T(8,128)(2,1)S(1)} %copy.84), channel_id=1, source_target_pairs={{15,0},{0,1},{1,2},{2,3},{3,4},{4,5},{5,6},{6,7},{7,8},{8,9},{9,10... | collective-permute-start | bytes 884744 | tf_op jit(solution)/shard_map/while/body/eval_jaxpr/ppermute | solution.py:12
  131.3 9.8 %collective-permute-start = (bf16[192,768]{1,0:T(8,128)(2,1)S(1)}, bf16[192,768]{1,0:T(8,128)(2,1)S(1)}, u32[]{:S(2)}, u32[]{:S(2)}) collective-permute-start(bf16[192,768]{1,0:T(8,128)(2,1)S(1)} %copy.84), channel_id=1, source_target_pairs={{15,0},{0,1},{1,2},{2,3},{3,4},{4,5},{5,6},{6,7},{7,8},{8,9},{9,10... | collective-permute-start | bytes 884744 | tf_op jit(solution)/shard_map/while/body/eval_jaxpr/ppermute | solution.py:12
  141.1 9.8 %collective-permute-start = (bf16[192,768]{1,0:T(8,128)(2,1)S(1)}, bf16[192,768]{1,0:T(8,128)(2,1)S(1)}, u32[]{:S(2)}, u32[]{:S(2)}) collective-permute-start(bf16[192,768]{1,0:T(8,128)(2,1)S(1)} %copy.84), channel_id=1, source_target_pairs={{15,0},{0,1},{1,2},{2,3},{3,4},{4,5},{5,6},{6,7},{7,8},{8,9},{9,10... | collective-permute-start | bytes 884744 | tf_op jit(solution)/shard_map/while/body/eval_jaxpr/ppermute | solution.py:12
  151.0 9.8 %collective-permute-start = (bf16[192,768]{1,0:T(8,128)(2,1)S(1)}, bf16[192,768]{1,0:T(8,128)(2,1)S(1)}, u32[]{:S(2)}, u32[]{:S(2)}) collective-permute-start(bf16[192,768]{1,0:T(8,128)(2,1)S(1)} %copy.84), channel_id=1, source_target_pairs={{15,0},{0,1},{1,2},{2,3},{3,4},{4,5},{5,6},{6,7},{7,8},{8,9},{9,10... | collective-permute-start | bytes 884744 | tf_op jit(solution)/shard_map/while/body/eval_jaxpr/ppermute | solution.py:12
  170.7 9.8 %collective-permute-start = (bf16[192,768]{1,0:T(8,128)(2,1)S(1)}, bf16[192,768]{1,0:T(8,128)(2,1)S(1)}, u32[]{:S(2)}, u32[]{:S(2)}) collective-permute-start(bf16[192,768]{1,0:T(8,128)(2,1)S(1)} %copy.84), channel_id=1, source_target_pairs={{15,0},{0,1},{1,2},{2,3},{3,4},{4,5},{5,6},{6,7},{7,8},{8,9},{9,10... | collective-permute-start | bytes 884744 | tf_op jit(solution)/shard_map/while/body/eval_jaxpr/ppermute | solution.py:12
  180.6 9.8 %collective-permute-start = (bf16[192,768]{1,0:T(8,128)(2,1)S(1)}, bf16[192,768]{1,0:T(8,128)(2,1)S(1)}, u32[]{:S(2)}, u32[]{:S(2)}) collective-permute-start(bf16[192,768]{1,0:T(8,128)(2,1)S(1)} %copy.84), channel_id=1, source_target_pairs={{15,0},{0,1},{1,2},{2,3},{3,4},{4,5},{5,6},{6,7},{7,8},{8,9},{9,10... | collective-permute-start | bytes 884744 | tf_op jit(solution)/shard_map/while/body/eval_jaxpr/ppermute | solution.py:12
  190.4 9.8 %collective-permute-start = (bf16[192,768]{1,0:T(8,128)(2,1)S(1)}, bf16[192,768]{1,0:T(8,128)(2,1)S(1)}, u32[]{:S(2)}, u32[]{:S(2)}) collective-permute-start(bf16[192,768]{1,0:T(8,128)(2,1)S(1)} %copy.84), channel_id=1, source_target_pairs={{15,0},{0,1},{1,2},{2,3},{3,4},{4,5},{5,6},{6,7},{7,8},{8,9},{9,10... | collective-permute-start | bytes 884744 | tf_op jit(solution)/shard_map/while/body/eval_jaxpr/ppermute | solution.py:12
  200.3 9.8 %collective-permute-start = (bf16[192,768]{1,0:T(8,128)(2,1)S(1)}, bf16[192,768]{1,0:T(8,128)(2,1)S(1)}, u32[]{:S(2)}, u32[]{:S(2)}) collective-permute-start(bf16[192,768]{1,0:T(8,128)(2,1)S(1)} %copy.84), channel_id=1, source_target_pairs={{15,0},{0,1},{1,2},{2,3},{3,4},{4,5},{5,6},{6,7},{7,8},{8,9},{9,10... | collective-permute-start | bytes 884744 | tf_op jit(solution)/shard_map/while/body/eval_jaxpr/ppermute | solution.py:12
  324.4 13.2 %collective-permute-start.1 = (f32[192,768]{1,0:T(8,128)}, f32[192,768]{1,0:T(8,128)}, u32[]{:S(2)}, u32[]{:S(2)}) collective-permute-start(f32[192,768]{1,0:T(8,128)} %convolution_add_fusion.2), channel_id=1, source_target_pairs={{15,0},{0,1},{1,2},{2,3},{3,4},{4,5},{5,6},{6,7},{7,8},{8,9},{9,10... | collective-permute-start | bytes 1769480 | tf_op jit(solution)/shard_map/while/body/eval_jaxpr/ppermute | solution.py:12
  342.7 13.2 %collective-permute-start.1 = (f32[192,768]{1,0:T(8,128)}, f32[192,768]{1,0:T(8,128)}, u32[]{:S(2)}, u32[]{:S(2)}) collective-permute-start(f32[192,768]{1,0:T(8,128)} %convolution_add_fusion.2), channel_id=1, source_target_pairs={{15,0},{0,1},{1,2},{2,3},{3,4},{4,5},{5,6},{6,7},{7,8},{8,9},{9,10... | collective-permute-start | bytes 1769480 | tf_op jit(solution)/shard_map/while/body/eval_jaxpr/ppermute | solution.py:12
  361.0 13.2 %collective-permute-start.1 = (f32[192,768]{1,0:T(8,128)}, f32[192,768]{1,0:T(8,128)}, u32[]{:S(2)}, u32[]{:S(2)}) collective-permute-start(f32[192,768]{1,0:T(8,128)} %convolution_add_fusion.2), channel_id=1, source_target_pairs={{15,0},{0,1},{1,2},{2,3},{3,4},{4,5},{5,6},{6,7},{7,8},{8,9},{9,10... | collective-permute-start | bytes 1769480 | tf_op jit(solution)/shard_map/while/body/eval_jaxpr/ppermute | solution.py:12
  379.3 13.2 %collective-permute-start.1 = (f32[192,768]{1,0:T(8,128)}, f32[192,768]{1,0:T(8,128)}, u32[]{:S(2)}, u32[]{:S(2)}) collective-permute-start(f32[192,768]{1,0:T(8,128)} %convolution_add_fusion.2), channel_id=1, source_target_pairs={{15,0},{0,1},{1,2},{2,3},{3,4},{4,5},{5,6},{6,7},{7,8},{8,9},{9,10... | collective-permute-start | bytes 1769480 | tf_op jit(solution)/shard_map/while/body/eval_jaxpr/ppermute | solution.py:12
  397.6 13.2 %collective-permute-start.1 = (f32[192,768]{1,0:T(8,128)}, f32[192,768]{1,0:T(8,128)}, u32[]{:S(2)}, u32[]{:S(2)}) collective-permute-start(f32[192,768]{1,0:T(8,128)} %convolution_add_fusion.2), channel_id=1, source_target_pairs={{15,0},{0,1},{1,2},{2,3},{3,4},{4,5},{5,6},{6,7},{7,8},{8,9},{9,10... | collective-permute-start | bytes 1769480 | tf_op jit(solution)/shard_map/while/body/eval_jaxpr/ppermute | solution.py:12
  415.9 13.2 %collective-permute-start.1 = (f32[192,768]{1,0:T(8,128)}, f32[192,768]{1,0:T(8,128)}, u32[]{:S(2)}, u32[]{:S(2)}) collective-permute-start(f32[192,768]{1,0:T(8,128)} %convolution_add_fusion.2), channel_id=1, source_target_pairs={{15,0},{0,1},{1,2},{2,3},{3,4},{4,5},{5,6},{6,7},{7,8},{8,9},{9,10... | collective-permute-start | bytes 1769480 | tf_op jit(solution)/shard_map/while/body/eval_jaxpr/ppermute | solution.py:12
  434.2 13.2 %collective-permute-start.1 = (f32[192,768]{1,0:T(8,128)}, f32[192,768]{1,0:T(8,128)}, u32[]{:S(2)}, u32[]{:S(2)}) collective-permute-start(f32[192,768]{1,0:T(8,128)} %convolution_add_fusion.2), channel_id=1, source_target_pairs={{15,0},{0,1},{1,2},{2,3},{3,4},{4,5},{5,6},{6,7},{7,8},{8,9},{9,10... | collective-permute-start | bytes 1769480 | tf_op jit(solution)/shard_map/while/body/eval_jaxpr/ppermute | solution.py:12
  452.5 13.2 %collective-permute-start.1 = (f32[192,768]{1,0:T(8,128)}, f32[192,768]{1,0:T(8,128)}, u32[]{:S(2)}, u32[]{:S(2)}) collective-permute-start(f32[192,768]{1,0:T(8,128)} %convolution_add_fusion.2), channel_id=1, source_target_pairs={{15,0},{0,1},{1,2},{2,3},{3,4},{4,5},{5,6},{6,7},{7,8},{8,9},{9,10... | collective-permute-start | bytes 1769480 | tf_op jit(solution)/shard_map/while/body/eval_jaxpr/ppermute | solution.py:12
  470.8 13.2 %collective-permute-start.1 = (f32[192,768]{1,0:T(8,128)}, f32[192,768]{1,0:T(8,128)}, u32[]{:S(2)}, u32[]{:S(2)}) collective-permute-start(f32[192,768]{1,0:T(8,128)} %convolution_add_fusion.2), channel_id=1, source_target_pairs={{15,0},{0,1},{1,2},{2,3},{3,4},{4,5},{5,6},{6,7},{7,8},{8,9},{9,10... | collective-permute-start | bytes 1769480 | tf_op jit(solution)/shard_map/while/body/eval_jaxpr/ppermute | solution.py:12
  489.1 13.2 %collective-permute-start.1 = (f32[192,768]{1,0:T(8,128)}, f32[192,768]{1,0:T(8,128)}, u32[]{:S(2)}, u32[]{:S(2)}) collective-permute-start(f32[192,768]{1,0:T(8,128)} %convolution_add_fusion.2), channel_id=1, source_target_pairs={{15,0},{0,1},{1,2},{2,3},{3,4},{4,5},{5,6},{6,7},{7,8},{8,9},{9,10... | collective-permute-start | bytes 1769480 | tf_op jit(solution)/shard_map/while/body/eval_jaxpr/ppermute | solution.py:12
  507.4 13.2 %collective-permute-start.1 = (f32[192,768]{1,0:T(8,128)}, f32[192,768]{1,0:T(8,128)}, u32[]{:S(2)}, u32[]{:S(2)}) collective-permute-start(f32[192,768]{1,0:T(8,128)} %convolution_add_fusion.2), channel_id=1, source_target_pairs={{15,0},{0,1},{1,2},{2,3},{3,4},{4,5},{5,6},{6,7},{7,8},{8,9},{9,10... | collective-permute-start | bytes 1769480 | tf_op jit(solution)/shard_map/while/body/eval_jaxpr/ppermute | solution.py:12
  525.7 13.2 %collective-permute-start.1 = (f32[192,768]{1,0:T(8,128)}, f32[192,768]{1,0:T(8,128)}, u32[]{:S(2)}, u32[]{:S(2)}) collective-permute-start(f32[192,768]{1,0:T(8,128)} %convolution_add_fusion.2), channel_id=1, source_target_pairs={{15,0},{0,1},{1,2},{2,3},{3,4},{4,5},{5,6},{6,7},{7,8},{8,9},{9,10... | collective-permute-start | bytes 1769480 | tf_op jit(solution)/shard_map/while/body/eval_jaxpr/ppermute | solution.py:12
  544.0 13.2 %collective-permute-start.1 = (f32[192,768]{1,0:T(8,128)}, f32[192,768]{1,0:T(8,128)}, u32[]{:S(2)}, u32[]{:S(2)}) collective-permute-start(f32[192,768]{1,0:T(8,128)} %convolution_add_fusion.2), channel_id=1, source_target_pairs={{15,0},{0,1},{1,2},{2,3},{3,4},{4,5},{5,6},{6,7},{7,8},{8,9},{9,10... | collective-permute-start | bytes 1769480 | tf_op jit(solution)/shard_map/while/body/eval_jaxpr/ppermute | solution.py:12
  562.3 13.2 %collective-permute-start.1 = (f32[192,768]{1,0:T(8,128)}, f32[192,768]{1,0:T(8,128)}, u32[]{:S(2)}, u32[]{:S(2)}) collective-permute-start(f32[192,768]{1,0:T(8,128)} %convolution_add_fusion.2), channel_id=1, source_target_pairs={{15,0},{0,1},{1,2},{2,3},{3,4},{4,5},{5,6},{6,7},{7,8},{8,9},{9,10... | collective-permute-start | bytes 1769480 | tf_op jit(solution)/shard_map/while/body/eval_jaxpr/ppermute | solution.py:12
  580.6 13.2 %collective-permute-start.1 = (f32[192,768]{1,0:T(8,128)}, f32[192,768]{1,0:T(8,128)}, u32[]{:S(2)}, u32[]{:S(2)}) collective-permute-start(f32[192,768]{1,0:T(8,128)} %convolution_add_fusion.2), channel_id=1, source_target_pairs={{15,0},{0,1},{1,2},{2,3},{3,4},{4,5},{5,6},{6,7},{7,8},{8,9},{9,10... | collective-permute-start | bytes 1769480 | tf_op jit(solution)/shard_map/while/body/eval_jaxpr/ppermute | solution.py:12
  598.9 13.2 %collective-permute-start.1 = (f32[192,768]{1,0:T(8,128)}, f32[192,768]{1,0:T(8,128)}, u32[]{:S(2)}, u32[]{:S(2)}) collective-permute-start(f32[192,768]{1,0:T(8,128)} %convolution_add_fusion.2), channel_id=1, source_target_pairs={{15,0},{0,1},{1,2},{2,3},{3,4},{4,5},{5,6},{6,7},{7,8},{8,9},{9,10... | collective-permute-start | bytes 1769480 | tf_op jit(solution)/shard_map/while/body/eval_jaxpr/ppermute | solution.py:12
  627.4 35.1 %all-to-all-start.2 = ((f32[128,3,768]{2,1,0:T(4,128)}), f32[128,3,768]{2,1,0:T(4,128)S(1)}, u32[]{:S(2)}, u32[]{:S(2)}) async-start(f32[128,3,768]{2,1,0:T(4,128)} %copy.48), calls=%async_computation.2 | async-start | bytes 3145728 | tf_op jit(solution)/shard_map/all_to_all | solution.py:147
  (45 other events, 688.7 us)
Sparse Core Ops, SparseCore 0:
  614.4 212.5 all-reduce.1
where the time goes:
time: 846 us; the launch traced here: 841 us
  waiting for transfers between devices  394 us (47%)
  matrix products  182 us (22%)
  blocking collectives  106 us (13%)
  local copies, waits for them, and re-layouts  83.5 us (10%)
  other arithmetic  49.2 us (6%)
  between operations  14.4 us (2%)
  starting transfers between devices  10.6 us (1%)
    ppermute x31, waiting for transfers between devices, shifted(): return lax.ppermute(block, axis, route)  192 us
    psum x1, waiting for transfers between devices, shards(): source_grad = lax.psum(source_acc, 'grp')  159 us
    all_gather x3, blocking collectives, merged(): pieces = jax.tree.map(lambda part: lax.all_gather(part, axis), value)  85.1 us
    dot_general x16, matrix products, backward(): jnp.einsum('rt,td->rd', prob_tile, tgt_block, preferred_element_type=jnp....  85 us
    dot_general x32, matrix products, adjusted_scores(): jnp.einsum('rd,td->rt', source_emb, tgt_block, preferred_element_type=jnp...  57.1 us
    dot_general x16, matrix products, backward(): jnp.einsum('rt,rd->td', prob_tile, source_emb, preferred_element_type=jnp...  40.2 us
    all_to_all x1, waiting for transfers between devices, shards(): lax.all_to_all(outgoing, ('grp', 'blk'), split_axis=0, concat_axis=0, til...  30.3 us
    add x16, other arithmetic, absorb(): positive_sum + jnp.sum(jnp.where(positive, adjusted, 0.0), axis=1)  21 us
  transfers between devices with their start and end apart: 34, of which 34 were waited for; matrix products, arithmetic and copies ran while one was open for 22% of the time, Pallas kernels for 0%

commit v1 on v0

v1 whole, which is shorter than its diff:
```python
import jax
import jax.numpy as jnp
from jax import lax
from jax.experimental import pallas as pl
from jax.experimental.pallas import tpu as pltpu
from jax.sharding import PartitionSpec as P

BF, F32 = jnp.bfloat16, jnp.float32
NEG = -1e30
LOW = -3e38
TILE = 384
CHUNKS = (((0, 0), (0, 1)), ((1, 0), (3, 0)), ((2, 0), (1, 1)), ((3, 1), (2, 1)))


def hop_blk(value, dz, dy, dc):
    route = []
    for i in range(16):
        z, y, c = i // 4, (i // 2) % 2, i % 2
        route.append((i, ((z + dz) % 4) * 4 + (y ^ dy) * 2 + (c ^ dc)))
    return lax.ppermute(value, "blk", route)


def hop_grp(value, dx, dy):
    return lax.ppermute(value, "grp", [(i, ((i // 2 + dx) % 4) * 2 + ((i % 2) ^ dy)) for i in range(8)])


def dot_f32(a, b, dims):
    return lax.dot_general(a, b, (dims, ((), ())), preferred_element_type=F32)


def columns_of(rows):
    pad = jnp.zeros((120, rows.shape[1]), F32)
    return jnp.transpose(jnp.concatenate([rows, pad], axis=0))


def score_kernel(place, src, t0, t1, t2, t3, e_out, stat_out, tgt_out, s_ref, d_ref, a_ref):
    rows = t0.shape[0]
    step = pl.program_id(0)

    @pl.when(step == 0)
    def _():
        top = jnp.zeros((1, 1), F32)
        for q, t in enumerate((t0, t1, t2, t3)):
            block = t[...]
            tgt_out[pl.ds(q * rows, rows), :] = block
            top = jnp.maximum(top, jnp.max(jnp.abs(block.astype(F32)), keepdims=True))
        a_ref[...] = jnp.broadcast_to(top, a_ref.shape)

    tgt = tgt_out[...]
    lane = lax.broadcasted_iota(jnp.int32, (rows, 128), 1)
    for sub in range(2):
        here = pl.ds(sub * rows, rows)
        s_ref[sub] = dot_f32(src[here, :], tgt, ((1,), (1,)))
        d_ref[sub] = jnp.zeros((rows, 1), F32)
        for q in range(4):

            @pl.when(place[q] == step * 2 + sub)
            def _():
                s = s_ref[sub]
                ahead = lax.broadcasted_iota(jnp.int32, s.shape, 1) - lax.broadcasted_iota(jnp.int32, s.shape, 0)
                mask = ahead == q * rows
                d_ref[sub] = jnp.sum(jnp.where(mask, s, 0.0), axis=1, keepdims=True)
                s_ref[sub] = jnp.where(mask, NEG, s)

    parts = []
    for sub in range(2):
        s = s_ref[sub]
        top = jnp.max(s, axis=1, keepdims=True)
        e = jnp.exp(s - top)
        total = jnp.sum(e, axis=1, keepdims=True)
        e_out[pl.ds(sub * rows, rows), :] = e.astype(BF)
        part = jnp.where(lane == 0, top, jnp.where(lane == 1, total, jnp.where(lane == 2, d_ref[sub], a_ref[0:1, :])))
        parts.append(part)
    stat_out[...] = jnp.transpose(jnp.concatenate(parts, axis=0))[0:8, :]


def score_call(place, src, blocks):
    rows, width = blocks[0].shape
    total = src.shape[0]
    cols = 4 * rows
    whole = pl.BlockSpec((rows, width), lambda i, p: (0, 0))
    return pl.pallas_call(
        score_kernel,
        out_shape=(
            jax.ShapeDtypeStruct((total, cols), BF),
            jax.ShapeDtypeStruct((8, total), F32),
            jax.ShapeDtypeStruct((cols, width), BF),
        ),
        grid_spec=pltpu.PrefetchScalarGridSpec(
            num_scalar_prefetch=1,
            grid=(total // TILE,),
            in_specs=[pl.BlockSpec((TILE, width), lambda i, p: (i, 0))] + [whole] * 4,
            out_specs=(
                pl.BlockSpec((TILE, cols), lambda i, p: (i, 0)),
                pl.BlockSpec((8, TILE), lambda i, p: (0, i)),
                pl.BlockSpec((cols, width), lambda i, p: (0, 0)),
            ),
            scratch_shapes=[
                pltpu.VMEM((2, rows, cols), F32),
                pltpu.VMEM((2, rows, 1), F32),
                pltpu.VMEM((8, 128), F32),
            ],
        ),
        compiler_params=pltpu.CompilerParams(vmem_limit_bytes=40 << 20),
        cost_estimate=pl.CostEstimate(
            flops=2 * total * cols * width, bytes_accessed=total * (width + cols) * 2, transcendentals=total * cols
        ),
        name="scores",
    )(place, src, *blocks)


def source_kernel(place, w_ref, *refs):
    es, tgts, out, acc = refs[0:4], refs[4:8], refs[8], refs[9]
    step = pl.program_id(0)
    rows = acc.shape[1]
    weights = columns_of(w_ref[...])
    for sub in range(2):
        here = slice(sub * rows, (sub + 1) * rows)
        total = None
        for c in range(4):
            part = dot_f32(es[c][here, :], tgts[c][...], ((1,), (0,))) * weights[here, c : c + 1]
            total = part if total is None else total + part
        acc[sub] = total
        at = place[step * 2 + sub]
        for c in range(4):

            @pl.when(at // 4 == c)
            def _():
                mine = tgts[c][pl.ds(pl.multiple_of((at % 4) * rows, rows), rows), :]
                acc[sub] = acc[sub] + weights[here, 4:5] * mine.astype(F32)

        out[here, :] = acc[sub].astype(BF)


def source_call(place, weights, es, tgts, rows):
    total, cols = es[0].shape
    width = tgts[0].shape[1]
    return pl.pallas_call(
        source_kernel,
        out_shape=jax.ShapeDtypeStruct((total, width), BF),
        grid_spec=pltpu.PrefetchScalarGridSpec(
            num_scalar_prefetch=1,
            grid=(total // TILE,),
            in_specs=[pl.BlockSpec((8, TILE), lambda i, p: (0, i))]
            + [pl.BlockSpec((TILE, cols), lambda i, p: (i, 0))] * 4
            + [pl.BlockSpec((cols, width), lambda i, p: (0, 0))] * 4,
            out_specs=pl.BlockSpec((TILE, width), lambda i, p: (i, 0)),
            scratch_shapes=[pltpu.VMEM((2, rows, width), F32)],
        ),
        compiler_params=pltpu.CompilerParams(vmem_limit_bytes=40 << 20),
        cost_estimate=pl.CostEstimate(
            flops=8 * total * cols * width, bytes_accessed=total * (4 * cols + width) * 2, transcendentals=0
        ),
        name="source_terms",
    )(place, weights, *es, *tgts)


def target_kernel(place, w_ref, e_ref, src_ref, keep, give, acc, scaled, *, chunk):
    step, steps = pl.program_id(0), pl.num_programs(0)
    rows = src_ref.shape[0] // 2
    weights = columns_of(w_ref[...])
    scaled[...] = (src_ref[...].astype(F32) * weights[:, chunk : chunk + 1]).astype(BF)
    part = dot_f32(e_ref[...], scaled[...], ((0,), (0,)))

    @pl.when(step == 0)
    def _():
        acc[...] = part

    @pl.when(step > 0)
    def _():
        acc[...] = acc[...] + part

    for sub in range(2):
        here = slice(sub * rows, (sub + 1) * rows)
        for q in range(4):

            @pl.when(place[q] == step * 2 + sub)
            def _():
                there = pl.ds(q * rows, rows)
                acc[there, :] = acc[there, :] + weights[here, 4:5] * src_ref[here, :].astype(F32)

    @pl.when(step == steps - 1)
    def _():
        keep[...] = acc[0 : 2 * rows, :]
        give[...] = acc[2 * rows : 4 * rows, :]


def target_call(place, weights, e, src, chunk):
    total, cols = e.shape
    width = src.shape[1]
    half = jax.ShapeDtypeStruct((cols // 2, width), F32)
    half_spec = pl.BlockSpec((cols // 2, width), lambda i, p: (0, 0))

    def kernel(*refs):
        target_kernel(*refs, chunk=chunk)

    return pl.pallas_call(
        kernel,
        out_shape=(half, half),
        grid_spec=pltpu.PrefetchScalarGridSpec(
            num_scalar_prefetch=1,
            grid=(total // TILE,),
            in_specs=[
                pl.BlockSpec((8, TILE), lambda i, p: (0, i)),
                pl.BlockSpec((TILE, cols), lambda i, p: (i, 0)),
                pl.BlockSpec((TILE, width), lambda i, p: (i, 0)),
            ],
            out_specs=(half_spec, half_spec),
            scratch_shapes=[pltpu.VMEM((cols, width), F32), pltpu.VMEM((TILE, width), BF)],
        ),
        compiler_params=pltpu.CompilerParams(vmem_limit_bytes=40 << 20),
        cost_estimate=pl.CostEstimate(
            flops=2 * total * cols * width, bytes_accessed=total * (width + cols) * 2 + cols * width * 4, transcendentals=0
        ),
        name="target_terms",
    )(place, weights, e, src)


def shards(source_emb, target_emb, hard_pool, hard_index, language, margin):
    total, width = source_emb.shape
    rows = target_emb.shape[0]
    blk, grp = lax.axis_index("blk"), lax.axis_index("grp")
    owners = 128
    cap = max(2, (2 * rows + owners - 1) // owners)
    slots = owners * cap
    z, y, c = blk // 4, (blk // 2) % 2, blk % 2

    start = grp * rows
    own_index = lax.dynamic_slice_in_dim(hard_index, start, rows, 0)
    own_source = lax.dynamic_slice_in_dim(source_emb, start, rows, 0)
    owner, pool_row = own_index // rows, own_index % rows
    position = jnp.arange(rows, dtype=jnp.int32)
    same = (owner[:, None] == owner[None, :]) & (position[None, :] < position[:, None])
    slot = owner * cap + jnp.sum(same.astype(jnp.int32), axis=1)
    at_slot = slot[:, None] == jnp.arange(slots, dtype=jnp.int32)[None, :]
    requests = jnp.sum(jnp.where(at_slot, pool_row[:, None] + 1, 0), axis=0) - 1
    wanted = lax.all_to_all(requests.reshape(owners, cap), ("grp", "blk"), 0, 0, tiled=True).reshape(slots)
    serve = (wanted[:, None] == position[None, :]).astype(BF)
    served = dot_f32(serve, hard_pool, ((1,), (0,))).astype(BF).reshape(owners, cap, width)
    fetched = lax.all_to_all(served, ("grp", "blk"), 0, 0, tiled=True).reshape(slots, width)
    pick = at_slot.astype(BF)
    hard_rows = dot_f32(pick, fetched, ((1,), (0,)))
    hard_score = jnp.sum(own_source.astype(F32) * hard_rows, axis=1)

    lang_match = language[:, None] == jnp.arange(margin.shape[0], dtype=jnp.int32)[None, :]
    margin_row = jnp.sum(jnp.where(lang_match, margin[None, :], 0.0), axis=1)

    have = {(0, 0, 0): target_emb}
    have[0, 1, 0] = hop_blk(target_emb, 0, 1, 0)
    for dz in (1, 3, 2):
        have[dz, 0, 0] = hop_blk(target_emb, -dz, 0, 0)
    for dz in (1, 3, 2):
        have[dz, 1, 0] = hop_blk(have[0, 1, 0], -dz, 0, 0)
    for dz, dy in [pair for chunk in CHUNKS for pair in chunk]:
        have[dz, dy, 1] = hop_blk(have[dz, dy, 0], 0, 0, 1)

    holds = grp == blk // 2
    place = {}
    for dz in range(4):
        for dy in range(2):
            for dc in range(2):
                zz = (z + dz) % 4
                k = (zz % 2) * 4 + (y ^ dy) * 2 + (c ^ dc)
                place[dz, dy, dc] = jnp.where(holds & (zz // 2 == c), k, -1)
    order = [[(dz, dy, dc) for dc in (0, 1) for dz, dy in chunk] for chunk in CHUNKS]
    places = [jnp.stack([place[key] for key in chunk]) for chunk in order]
    flat = jnp.concatenate(places)
    found = flat[None, :] == jnp.arange(8, dtype=jnp.int32)[:, None]
    where_is = jnp.sum(jnp.where(found, jnp.arange(16, dtype=jnp.int32)[None, :] + 1, 0), axis=1) - 1
    where_is = jnp.where(where_is < 0, -4, where_is)

    es, stats, tgts = [], [], []
    for chunk, at in zip(order, places):
        e, stat, tgt = score_call(at, source_emb, [have[key] for key in chunk])
        es.append(e)
        stats.append(stat)
        tgts.append(tgt)

    tops = jnp.stack([stat[0] for stat in stats])
    sums = jnp.stack([stat[1] for stat in stats])
    diag = sum(stat[2] for stat in stats)
    reach = jnp.maximum(jnp.max(jnp.stack([stat[3] for stat in stats]), axis=0), jnp.max(jnp.abs(hard_rows)))
    pos = jnp.where(holds, diag - margin_row, 0.0)
    hard_all = lax.dynamic_update_slice_in_dim(jnp.full((total,), LOW, F32), hard_score, start, 0)
    top = jnp.maximum(jnp.max(tops, axis=0), hard_all)
    off = jnp.sum(sums * jnp.exp(tops - top), axis=0) + jnp.exp(hard_all - top)
    mine = jnp.stack([top, off, pos, reach])
    everyone = lax.all_to_all(jnp.broadcast_to(mine[None], (8, 4, total)), "grp", 0, 0, tiled=True)
    pos = jnp.sum(everyone[:, 2], axis=0)
    reach = jnp.max(everyone[:, 3], axis=0)
    top = jnp.maximum(jnp.max(everyone[:, 0], axis=0), pos)
    off = jnp.sum(everyone[:, 1] * jnp.exp(everyone[:, 0] - top), axis=0)
    log_total = top + jnp.log(off + jnp.exp(pos - top))
    row_loss = log_total - pos
    less = jnp.exp(pos - log_total) - 1.0
    weights = jnp.exp(tops - log_total)
    diag_weight = jnp.where(holds, less, 0.0)
    weights = jnp.concatenate([weights, diag_weight[None], jnp.zeros((3, total), F32)])

    source_part = source_call(where_is, weights, es, tgts, rows)
    source_parts = lax.all_to_all(source_part.reshape(8, rows, width), "grp", 0, 0, tiled=True)
    own_total = lax.dynamic_slice_in_dim(log_total, start, rows, 0)
    hard_prob = jnp.exp(hard_score - own_total)
    own_grad = jnp.sum(source_parts.astype(F32), axis=0) + hard_prob[:, None] * hard_rows
    mass = jnp.abs(less) + off * jnp.exp(top - log_total)
    bound = jnp.maximum(1.01 * reach * mass, 1e-30)
    own_bound = lax.dynamic_slice_in_dim(bound, start, rows, 0)
    coded = jnp.round(jnp.clip(own_grad * (32767.0 / own_bound)[:, None], -32767.0, 32767.0)).astype(jnp.int16)
    pair = jnp.stack([coded, hop_grp(coded, 0, 1)])
    pairs = [pair] + [hop_grp(pair, -dx, 0) for dx in (1, 2, 3)]
    x_at, y_at = grp // 2, grp % 2
    source_grad = jnp.zeros((total, width), F32)
    for dx in range(4):
        for dy in range(2):
            at = (((x_at + dx) % 4) * 2 + (y_at ^ dy)) * rows
            scale = lax.dynamic_slice_in_dim(bound, at, rows, 0) * (1.0 / 32767.0)
            source_grad = lax.dynamic_update_slice_in_dim(
                source_grad, pairs[dx][dy].astype(F32) * scale[:, None], at, 0
            )

    part = {}
    for n, chunk in enumerate(CHUNKS):
        keep, give = target_call(places[n], weights, es[n], source_emb, n)
        both = keep + hop_blk(give, 0, 0, 1)
        part[chunk[0]], part[chunk[1]] = both[:rows], both[rows:]
    lines = [part[0, 0], part[0, 1]]
    for dz in (1, 3, 2):
        moved = [hop_blk(part[dz, dy].astype(BF), dz, 0, 0).astype(F32) for dy in range(2)]
        lines = [lines[0] + moved[0], lines[1] + moved[1]]
    target_grad = lines[0] + hop_blk(lines[1], 0, 1, 0)

    contribution = (hard_prob[:, None] * own_source.astype(F32)).astype(BF)
    outgoing = dot_f32(pick, contribution, ((0,), (0,))).astype(BF).reshape(owners, cap, width)
    incoming = lax.all_to_all(outgoing, ("grp", "blk"), 0, 0, tiled=True).reshape(slots, width)
    pool_grad = dot_f32(serve, incoming, ((0,), (0,)))
    return (row_loss, source_grad, target_grad, pool_grad)


def solution(mesh):
    in_specs = (P("blk", None), P(("grp", "blk"), None), P(("grp", "blk"), None), P("blk"), P("blk"), P())
    out_specs = (P("blk"), P("blk", None), P(("grp", "blk"), None), P(("grp", "blk"), None))
    return jax.shard_map(shards, mesh=mesh, in_specs=in_specs, out_specs=out_specs, check_vma=False)
```

time: 846 us -> 288 us (0.34)
  waiting for transfers between devices: 394 us -> 66.7 us
  matrix products: 182 us -> 6.56 us
  blocking collectives: 106 us -> 0 us
  Pallas kernels: 0 us -> 78.2 us
  starting transfers between devices: 10.6 us -> 75.4 us
  local copies, waits for them, and re-layouts: 83.5 us -> 37.1 us
  other arithmetic: 49.2 us -> 17.6 us
  between operations: 14.4 us -> 1.8 us
    dot_general x64 -> x4, matrix products: 182 us -> 6.56 us  [dot_f32(): return lax.dot_general(a, b, (dims, ((), ())), preferred_element_type=F32)]
    psum x1 -> x0, waiting for transfers between devices: 159 us -> none  [shards(): source_grad = lax.psum(source_acc, 'grp')]
    ppermute x31 -> x30, waiting for transfers between devices: 192 us -> 38.6 us  [the longest x4 24.6 us: hop_grp(): lax.ppermute(value, 'grp', [(i, (i // 2 + dx) % 4 * 2 + (i % 2 ^ dy)) for...]
    all_gather x3 -> x0, blocking collectives: 85.1 us -> none  [merged(): pieces = jax.tree.map(lambda part: lax.all_gather(part, axis), value)]
    pallas_call x0 -> x9, Pallas kernels: none -> 78.2 us  [the longest x4 36.5 us: score_call(): pl.pallas_call(score_kernel, out_shape=(jax.ShapeDtypeStruct((total, cols...]
    ppermute x31 -> x30, starting transfers between devices: 1.16 us -> 38.4 us  [the longest x26 28.5 us: hop_blk(): return lax.ppermute(value, 'blk', route)]
    all_to_all x2 -> x5, starting transfers between devices: 9.4 us -> 37 us  [the longest x1 14.4 us: shards(): lax.all_to_all(source_part.reshape(8, rows, width), 'grp', 0, 0, tiled=True)]
    scatter x3 -> x0, local copies, waits for them, and re-layouts: 22.3 us -> none  [the longest x2 13 us: shards(): outgoing = jnp.zeros((owner_count, slot_cap, width), jnp.float32).at[owne...]
  transfers between devices with their start and end apart: 34 -> 35, of which waited for: 34 -> 8; matrix products, arithmetic and copies ran while one was open for 22% -> 11% of each run, Pallas kernels for 0% -> 24%
where the time goes in v1:
time: 288 us; the launch traced here: 283 us
  Pallas kernels  78.2 us (27%)
  starting transfers between devices  75.4 us (26%)
  waiting for transfers between devices  66.7 us (23%)
  local copies, waits for them, and re-layouts  37.1 us (13%)
  other arithmetic  17.6 us (6%)
  matrix products  6.56 us (2%)
    pallas_call x4, Pallas kernels, score_call(): pl.pallas_call(score_kernel, out_shape=(jax.ShapeDtypeStruct((total, cols...  36.5 us
    pallas_call x4, Pallas kernels, target_call(): pl.pallas_call(kernel, out_shape=(half, half), grid_spec=pltpu.PrefetchSc...  28.6 us
    ppermute x26, starting transfers between devices, hop_blk(): return lax.ppermute(value, 'blk', route)  28.5 us
    ppermute x4, waiting for transfers between devices, hop_grp(): lax.ppermute(value, 'grp', [(i, (i // 2 + dx) % 4 * 2 + (i % 2 ^ dy)) for...  24.6 us
    unnamed x80, local copies, waits for them, and re-layouts  23.8 us
    all_to_all x1, starting transfers between devices, shards(): lax.all_to_all(source_part.reshape(8, rows, width), 'grp', 0, 0, tiled=True)  14.4 us
    ppermute x26, waiting for transfers between devices, hop_blk(): return lax.ppermute(value, 'blk', route)  14 us
    pallas_call x1, Pallas kernels, source_call(): pl.pallas_call(source_kernel, out_shape=jax.ShapeDtypeStruct((total, widt...  13.1 us
  transfers between devices with their start and end apart: 35, of which 8 were waited for; matrix products, arithmetic and copies ran while one was open for 11% of the time, Pallas kernels for 24%

profile of v1, /device:TPU:0, one launch (start us, length us, event | category | flops | bytes accessed | tf_op | source)
XLA Modules:
  0.0 283.4 jit_solution(11926535818167577285)
XLA Ops:
  0.6 4.2 %collective-permute-start.3 = (bf16[192,768]{1,0:T(8,128)(2,1)}, bf16[192,768]{1,0:T(8,128)(2,1)}, u32[]{:S(2)}, u32[]{:S(2)}) collective-permute-start(bf16[192,768]{1,0:T(8,128)(2,1)} %t0.1), channel_id=1, source_target_pairs={{0,12},{1,13},{2,14},{3,15},{4,0},{5,1},{6,2},{7,3},{8,4},{9,5},{1... | collective-permute-start | bytes 884744 | tf_op jit(solution)/shard_map/ppermute | solution.py:20
  4.8 3.2 %collective-permute-start = (bf16[192,768]{1,0:T(8,128)(2,1)}, bf16[192,768]{1,0:T(8,128)(2,1)}, u32[]{:S(2)}, u32[]{:S(2)}) collective-permute-start(bf16[192,768]{1,0:T(8,128)(2,1)} %t0.1), channel_id=1, source_target_pairs={{0,2},{1,3},{2,0},{3,1},{4,6},{5,7},{6,4},{7,5},{8,10},{9,11},{10,... | collective-permute-start | bytes 884744 | tf_op jit(solution)/shard_map/ppermute | solution.py:20
  11.3 7.2 %all-to-all-start = ((s32[128,1,3]{2,1,0:T(1,128)}), s32[128,1,3]{2,1,0:T(1,128)S(1)}, u32[]{:S(2)}, u32[]{:S(2)}) async-start(s32[128,1,3]{2,1,0:T(1,128)} %bitcast.16), calls=%async_computation | async-start | bytes 131072 | tf_op jit(solution)/shard_map/all_to_all | solution.py:237
  18.8 9.0 %all-to-all-done = s32[128,1,3]{2,1,0:T(1,128)S(1)} async-done(((s32[128,1,3]{2,1,0:T(1,128)}), s32[128,1,3]{2,1,0:T(1,128)S(1)}, u32[]{:S(2)}, u32[]{:S(2)}) %all-to-all-start) | async-done | bytes 1568 | tf_op jit(solution)/shard_map/all_to_all | solution.py:237
  32.7 5.7 %all-to-all-start.1 = ((bf16[128,3,768]{2,1,0:T(4,128)(2,1)}), bf16[128,3,768]{2,1,0:T(4,128)(2,1)}, u32[]{:S(2)}, u32[]{:S(2)}) async-start(bf16[128,3,768]{2,1,0:T(4,128)(2,1)} %reshape.150), calls=%async_computation.1 | async-start | bytes 1572864 | tf_op jit(solution)/shard_map/all_to_all | solution.py:240
  39.1 3.0 %collective-permute-start.8 = (bf16[192,768]{1,0:T(8,128)(2,1)}, bf16[192,768]{1,0:T(8,128)(2,1)}, u32[]{:S(2)}, u32[]{:S(2)}) collective-permute-start(bf16[192,768]{1,0:T(8,128)(2,1)} %collective-permute-done.t1), channel_id=1, source_target_pairs={{0,12},{1,13},{2,14},{3,15},{4,0},{5,1},{6,2},{7,3},{8,4},{9,5},{1... | collective-permute-start | bytes 884744 | tf_op jit(solution)/shard_map/ppermute | solution.py:20
  42.4 12.0 %all-to-all-done.1 = bf16[128,3,768]{2,1,0:T(4,128)(2,1)} async-done(((bf16[128,3,768]{2,1,0:T(4,128)(2,1)}), bf16[128,3,768]{2,1,0:T(4,128)(2,1)}, u32[]{:S(2)}, u32[]{:S(2)}) %all-to-all-start.1) | async-done | bytes 589856 | tf_op jit(solution)/shard_map/all_to_all | solution.py:240
  54.4 2.2 reshape.151
  58.3 2.8 %fusion = (f32[192]{0:T(256)S(1)}, f32[]{:T(128)}, f32[192,768]{1,0:T(8,128)}) fusion(bf16[1536,768]{1,0:T(8,128)(2,1)S(1)} %copy-done.4, s32[]{:T(128)S(6)} %select_n.321, bf16[384,768]{1,0:T(8,128)(2,1)} %reshape.151, s32[192]{0:T(256)S(1)} %multiply_add_fusion), kind=kOutput, calls=%fused_computation.10 | convolution fusion | flops 114057024 | bytes 1476104 | tf_op jit(solution)/shard_map/dot_general | solution.py:28
  62.0 9.3 %scores.5 = (bf16[1536,768]{1,0:T(8,128)(2,1)S(1)}, f32[8,1536]{1,0:T(8,128)S(1)}, bf16[768,768]{1,0:T(8,128)(2,1)S(1)}) custom-call(s32[4]{0:T(128)S(1)} %pad_add_fusion.2.place.refs_0_, bf16[1536,768]{1,0:T(8,128)(2,1)S(1)} %copy-done.4, bf16[192,768]{1,0:T(8,128)(2,1)} %collective-permute-done.3.t0, bf16[192,768]{1,0:T(8,128)(2,1)} %collective-permute-done.4.t1, ...), custom_call_target="tpu_custom_call" | custom-call | flops 1811939328 | bytes 4718592 | tf_op jit(solution)/shard_map/scores/pallas_call | solution.py:82
  74.6 9.3 %scores.4 = (bf16[1536,768]{1,0:T(8,128)(2,1)S(1)}, f32[8,1536]{1,0:T(8,128)S(1)}, bf16[768,768]{1,0:T(8,128)(2,1)S(1)}) custom-call(s32[4]{0:T(128)S(1)} %pad_add_fusion.1.place.refs_0_, bf16[1536,768]{1,0:T(8,128)(2,1)S(1)} %copy-done.4, bf16[192,768]{1,0:T(8,128)(2,1)S(1)} %copy-done.6, bf16[192,768]{1,0:T(8,128)(2,1)} %collective-permute-done.t1, ...), custom_call_target="tpu_custom_call" | custom-call | flops 1811939328 | bytes 4718592 | tf_op jit(solution)/shard_map/scores/pallas_call | solution.py:82
  86.4 9.0 %scores.6 = (bf16[1536,768]{1,0:T(8,128)(2,1)S(1)}, f32[8,1536]{1,0:T(8,128)S(1)}, bf16[768,768]{1,0:T(8,128)(2,1)S(1)}) custom-call(s32[4]{0:T(128)S(1)} %pad_add_fusion.3.place.refs_0_, bf16[1536,768]{1,0:T(8,128)(2,1)S(1)} %copy-done.4, bf16[192,768]{1,0:T(8,128)(2,1)S(1)} %collective-permute-done.7.t0, bf16[192,768]{1,0:T(8,128)(2,1)} %collective-permute-done.8.t1, ...), custom_call_target="tpu_custom_call" | custom-call | flops 1811939328 | bytes 4718592 | tf_op jit(solution)/shard_map/scores/pallas_call | solution.py:82
  97.9 8.9 %scores.7 = (bf16[1536,768]{1,0:T(8,128)(2,1)S(1)}, f32[8,1536]{1,0:T(8,128)S(1)}, bf16[768,768]{1,0:T(8,128)(2,1)S(1)}) custom-call(s32[4]{0:T(128)S(1)} %pad_add_fusion.4.place.refs_0_, bf16[1536,768]{1,0:T(8,128)(2,1)S(1)} %copy-done.4, bf16[192,768]{1,0:T(8,128)(2,1)} %collective-permute-done.11.t0, bf16[192,768]{1,0:T(8,128)(2,1)} %collective-permute-done.12.t1, ...), custom_call_target="tpu_custom_call" | custom-call | flops 1811939328 | bytes 4718592 | tf_op jit(solution)/shard_map/scores/pallas_call | solution.py:82
  110.8 3.4 %all-to-all-start.2 = ((f32[8,4,1536]{2,1,0:T(4,128)}), f32[8,4,1536]{2,1,0:T(4,128)S(1)}, u32[]{:S(2)}, u32[]{:S(2)}) async-start(f32[8,4,1536]{2,1,0:T(4,128)} %broadcast_in_dim.59), calls=%async_computation.2 | async-start | bytes 393216 | tf_op jit(solution)/shard_map/all_to_all | solution.py:288
  114.3 7.0 %all-to-all-done.2 = f32[8,4,1536]{2,1,0:T(4,128)S(1)} async-done(((f32[8,4,1536]{2,1,0:T(4,128)}), f32[8,4,1536]{2,1,0:T(4,128)S(1)}, u32[]{:S(2)}, u32[]{:S(2)}) %all-to-all-start.2) | async-done | bytes 196640 | tf_op jit(solution)/shard_map/all_to_all | solution.py:288
  126.3 6.4 %all-to-all-start.4 = ((bf16[128,3,768]{2,1,0:T(4,128)(2,1)}), bf16[128,3,768]{2,1,0:T(4,128)(2,1)}, u32[]{:S(2)}, u32[]{:S(2)}) async-start(bf16[128,3,768]{2,1,0:T(4,128)(2,1)} %reshape.153), calls=%async_computation.4 | async-start | bytes 1572864 | tf_op jit(solution)/shard_map/all_to_all | solution.py:334
  134.4 6.9 %target_terms.7 = (f32[384,768]{1,0:T(8,128)S(1)}, f32[384,768]{1,0:T(8,128)}) custom-call(s32[4]{0:T(128)S(1)} %pad_add_fusion.4.place.refs_0_, f32[8,1536]{1,0:T(8,128)S(1)} %maximum_maximum_fusion.w_ref.refs_1_, bf16[1536,768]{1,0:T(8,128)(2,1)S(1)} %copy-done.17, bf16[1536,768]{1,0:T(8,128)(2,1)S(1)} %copy-done.4), custom_call_target="tpu_custom_call" | custom-call | flops 1811939328 | bytes 7077888 | tf_op jit(solution)/shard_map/target_terms/pallas_call | solution.py:197
  147.9 13.1 %source_terms.1 = bf16[1536,768]{1,0:T(8,128)(2,1)} custom-call(s32[8]{0:T(128)S(1)} %compare_select_fusion.place, f32[8,1536]{1,0:T(8,128)S(1)} %maximum_maximum_fusion.w_ref.refs_1_, bf16[1536,768]{1,0:T(8,128)(2,1)S(1)} %copy-done.11, bf16[1536,768]{1,0:T(8,128)(2,1)S(1)} %copy-done.8, bf16[1536,768]{1,0:T(8,128)(2,1)S(1)} %copy-done.14, ...), custom_call_target="tpu_custom_call" | custom-call | flops 7247757312 | bytes 11796480 | tf_op jit(solution)/shard_map/source_terms/pallas_call | solution.py:138
  161.0 14.4 %all-to-all-start.3 = ((bf16[8,192,768]{2,1,0:T(8,128)(2,1)}), bf16[8,192,768]{2,1,0:T(8,128)(2,1)}, u32[]{:S(2)}, u32[]{:S(2)}) async-start(bf16[8,192,768]{2,1,0:T(8,128)(2,1)} %bitcast.18), calls=%async_computation.3 | async-start | bytes 4718592 | tf_op jit(solution)/shard_map/all_to_all | solution.py:301
  177.1 7.1 %target_terms.6 = (f32[384,768]{1,0:T(8,128)S(1)}, f32[384,768]{1,0:T(8,128)}) custom-call(s32[4]{0:T(128)S(1)} %pad_add_fusion.3.place.refs_0_, f32[8,1536]{1,0:T(8,128)S(1)} %maximum_maximum_fusion.w_ref.refs_1_, bf16[1536,768]{1,0:T(8,128)(2,1)S(1)} %copy-done.15, bf16[1536,768]{1,0:T(8,128)(2,1)S(1)} %copy-done.4), custom_call_target="tpu_custom_call" | custom-call | flops 1811939328 | bytes 7077888 | tf_op jit(solution)/shard_map/target_terms/pallas_call | solution.py:197
  185.7 7.4 %target_terms.4 = (f32[384,768]{1,0:T(8,128)S(1)}, f32[384,768]{1,0:T(8,128)}) custom-call(s32[4]{0:T(128)S(1)} %pad_add_fusion.1.place.refs_0_, f32[8,1536]{1,0:T(8,128)S(1)} %maximum_maximum_fusion.w_ref.refs_1_, bf16[1536,768]{1,0:T(8,128)(2,1)S(1)} %copy-done.12, bf16[1536,768]{1,0:T(8,128)(2,1)S(1)} %copy-done.5), custom_call_target="tpu_custom_call" | custom-call | flops 1811939328 | bytes 7077888 | tf_op jit(solution)/shard_map/target_terms/pallas_call | solution.py:197
  193.1 7.2 %target_terms.5 = (f32[384,768]{1,0:T(8,128)S(1)}, f32[384,768]{1,0:T(8,128)}) custom-call(s32[4]{0:T(128)S(1)} %pad_add_fusion.2.place.refs_0_, f32[8,1536]{1,0:T(8,128)S(1)} %maximum_maximum_fusion.w_ref.refs_1_, bf16[1536,768]{1,0:T(8,128)(2,1)S(1)} %copy-done.9, bf16[1536,768]{1,0:T(8,128)(2,1)S(1)} %copy-done.5), custom_call_target="tpu_custom_call" | custom-call | flops 1811939328 | bytes 7077888 | tf_op jit(solution)/shard_map/target_terms/pallas_call | solution.py:197
  209.7 3.0 %collective-permute-start.24 = (bf16[192,768]{1,0:T(8,128)(2,1)}, bf16[192,768]{1,0:T(8,128)(2,1)S(1)}, u32[]{:S(2)}, u32[]{:S(2)}) collective-permute-start(bf16[192,768]{1,0:T(8,128)(2,1)} %get-tuple-element.53), channel_id=1, source_target_pairs={{0,8},{1,9},{2,10},{3,11},{4,12},{5,13},{6,14},{7,15},{8,0},{9,1},... | collective-permute-start | bytes 884744 | tf_op jit(solution)/shard_map/ppermute | solution.py:20
  213.5 2.5 add.456
  222.1 8.4 %collective-permute-done.25 = bf16[192,768]{1,0:T(8,128)(2,1)} collective-permute-done((bf16[192,768]{1,0:T(8,128)(2,1)}, bf16[192,768]{1,0:T(8,128)(2,1)}, u32[]{:S(2)}, u32[]{:S(2)}) %collective-permute-start.25) | collective-permute-done | bytes 294944 | tf_op jit(solution)/shard_map/ppermute | solution.py:20
  231.8 3.8 %collective-permute-start.29 = (f32[192,768]{1,0:T(8,128)S(1)}, f32[192,768]{1,0:T(8,128)S(1)}, u32[]{:S(2)}, u32[]{:S(2)}) collective-permute-start(f32[192,768]{1,0:T(8,128)S(1)} %fusion.3), channel_id=1, source_target_pairs={{0,2},{1,3},{2,0},{3,1},{4,6},{5,7},{6,4},{7,5},{8,10},{9,11},{10,... | collective-permute-start | bytes 1769480 | tf_op jit(solution)/shard_map/ppermute | solution.py:20
  235.7 3.2 %collective-permute-start.22 = (bf16[192,768]{1,0:T(8,128)(2,1)S(1)}, bf16[192,768]{1,0:T(8,128)(2,1)S(1)}, u32[]{:S(2)}, u32[]{:S(2)}) collective-permute-start(bf16[192,768]{1,0:T(8,128)(2,1)S(1)} %get-tuple-element.52), channel_id=1, source_target_pairs={{0,12},{1,13},{2,14},{3,15},{4,0},{5,1},{6,2},{7,3},{8,4},{9,5},{1... | collective-permute-start | bytes 884744 | tf_op jit(solution)/shard_map/ppermute | solution.py:20
  239.0 3.3 %collective-permute-start.16 = (s16[2,192,768]{2,1,0:T(8,128)(2,1)S(1)}, s16[2,192,768]{2,1,0:T(8,128)(2,1)S(1)}, u32[]{:S(2)}, u32[]{:S(2)}) collective-permute-start(s16[2,192,768]{2,1,0:T(8,128)(2,1)S(1)} %pad_add_fusion), channel_id=1, source_target_pairs={{0,96},{16,112},{32,0},{48,16},{64,32},{80,48},{96,64},{112,80},{1... | collective-permute-start | bytes 1769480 | tf_op jit(solution)/shard_map/ppermute | solution.py:24
  245.6 3.5 %collective-permute-done.29 = f32[192,768]{1,0:T(8,128)S(1)} collective-permute-done((f32[192,768]{1,0:T(8,128)S(1)}, f32[192,768]{1,0:T(8,128)S(1)}, u32[]{:S(2)}, u32[]{:S(2)}) %collective-permute-start.29) | collective-permute-done | bytes 589856 | tf_op jit(solution)/shard_map/ppermute | solution.py:20
  252.1 3.3 %collective-permute-start.17 = (s16[2,192,768]{2,1,0:T(8,128)(2,1)S(1)}, s16[2,192,768]{2,1,0:T(8,128)(2,1)S(1)}, u32[]{:S(2)}, u32[]{:S(2)}) collective-permute-start(s16[2,192,768]{2,1,0:T(8,128)(2,1)S(1)} %pad_add_fusion), channel_id=1, source_target_pairs={{0,64},{16,80},{32,96},{48,112},{64,0},{80,16},{96,32},{112,48},{1... | collective-permute-start | bytes 1769480 | tf_op jit(solution)/shard_map/ppermute | solution.py:24
  255.6 11.3 %collective-permute-done.16 = s16[2,192,768]{2,1,0:T(8,128)(2,1)S(1)} collective-permute-done((s16[2,192,768]{2,1,0:T(8,128)(2,1)S(1)}, s16[2,192,768]{2,1,0:T(8,128)(2,1)S(1)}, u32[]{:S(2)}, u32[]{:S(2)}) %collective-permute-start.16) | collective-permute-done | bytes 589856 | tf_op jit(solution)/shard_map/ppermute | solution.py:24
  267.2 13.3 %collective-permute-done.17 = s16[2,192,768]{2,1,0:T(8,128)(2,1)S(1)} collective-permute-done((s16[2,192,768]{2,1,0:T(8,128)(2,1)S(1)}, s16[2,192,768]{2,1,0:T(8,128)(2,1)S(1)}, u32[]{:S(2)}, u32[]{:S(2)}) %collective-permute-start.17) | collective-permute-done | bytes 589856 | tf_op jit(solution)/shard_map/ppermute | solution.py:24
  (197 shorter events, 67.2 us)
Async XLA Ops:
  0.6 38.1 %collective-permute-start.3 = (bf16[192,768]{1,0:T(8,128)(2,1)}, bf16[192,768]{1,0:T(8,128)(2,1)}, u32[]{:S(2)}, u32[]{:S(2)}) collective-permute-start(bf16[192,768]{1,0:T(8,128)(2,1)} %t0.1), channel_id=1, source_target_pairs={{0,12},{1,13},{2,14},{3,15},{4,0},{5,1},{6,2},{7,3},{8,4},{9,5},{1... | collective-permute-start | bytes 884744 | tf_op jit(solution)/shard_map/ppermute | solution.py:20
  4.8 51.8 %collective-permute-start.1 = (bf16[192,768]{1,0:T(8,128)(2,1)}, bf16[192,768]{1,0:T(8,128)(2,1)S(1)}, u32[]{:S(2)}, u32[]{:S(2)}) collective-permute-start(bf16[192,768]{1,0:T(8,128)(2,1)} %t0.1), channel_id=1, source_target_pairs={{0,1},{1,0},{2,3},{3,2},{4,5},{5,4},{6,7},{7,6},{8,9},{9,8},{10,11... | collective-permute-start | bytes 884744 | tf_op jit(solution)/shard_map/ppermute | solution.py:20
  4.8 34.3 %collective-permute-start = (bf16[192,768]{1,0:T(8,128)(2,1)}, bf16[192,768]{1,0:T(8,128)(2,1)}, u32[]{:S(2)}, u32[]{:S(2)}) collective-permute-start(bf16[192,768]{1,0:T(8,128)(2,1)} %t0.1), channel_id=1, source_target_pairs={{0,2},{1,3},{2,0},{3,1},{4,6},{5,7},{6,4},{7,5},{8,10},{9,11},{10,... | collective-permute-start | bytes 884744 | tf_op jit(solution)/shard_map/ppermute | solution.py:20
  8.0 50.1 %collective-permute-start.7 = (bf16[192,768]{1,0:T(8,128)(2,1)}, bf16[192,768]{1,0:T(8,128)(2,1)S(1)}, u32[]{:S(2)}, u32[]{:S(2)}) collective-permute-start(bf16[192,768]{1,0:T(8,128)(2,1)} %t0.1), channel_id=1, source_target_pairs={{0,8},{1,9},{2,10},{3,11},{4,12},{5,13},{6,14},{7,15},{8,0},{9,1},... | collective-permute-start | bytes 884744 | tf_op jit(solution)/shard_map/ppermute | solution.py:20
  8.1 34.0 %collective-permute-start.4 = (bf16[192,768]{1,0:T(8,128)(2,1)}, bf16[192,768]{1,0:T(8,128)(2,1)}, u32[]{:S(2)}, u32[]{:S(2)}) collective-permute-start(bf16[192,768]{1,0:T(8,128)(2,1)} %t0.1), channel_id=1, source_target_pairs={{0,4},{1,5},{2,6},{3,7},{4,8},{5,9},{6,10},{7,11},{8,12},{9,13},{1... | collective-permute-start | bytes 884744 | tf_op jit(solution)/shard_map/ppermute | solution.py:20
  11.3 16.6 %all-to-all-start = ((s32[128,1,3]{2,1,0:T(1,128)}), s32[128,1,3]{2,1,0:T(1,128)S(1)}, u32[]{:S(2)}, u32[]{:S(2)}) async-start(s32[128,1,3]{2,1,0:T(1,128)} %bitcast.16), calls=%async_computation | async-start | bytes 131072 | tf_op jit(solution)/shard_map/all_to_all | solution.py:237
  32.7 21.7 %all-to-all-start.1 = ((bf16[128,3,768]{2,1,0:T(4,128)(2,1)}), bf16[128,3,768]{2,1,0:T(4,128)(2,1)}, u32[]{:S(2)}, u32[]{:S(2)}) async-start(bf16[128,3,768]{2,1,0:T(4,128)(2,1)} %reshape.150), calls=%async_computation.1 | async-start | bytes 1572864 | tf_op jit(solution)/shard_map/all_to_all | solution.py:240
  38.8 19.4 %collective-permute-start.5 = (bf16[192,768]{1,0:T(8,128)(2,1)}, bf16[192,768]{1,0:T(8,128)(2,1)}, u32[]{:S(2)}, u32[]{:S(2)}) collective-permute-start(bf16[192,768]{1,0:T(8,128)(2,1)} %collective-permute-done.3.t0), channel_id=1, source_target_pairs={{0,1},{1,0},{2,3},{3,2},{4,5},{5,4},{6,7},{7,6},{8,9},{9,8},{10,11... | collective-permute-start | bytes 884744 | tf_op jit(solution)/shard_map/ppermute | solution.py:20
  39.1 22.2 %collective-permute-start.8 = (bf16[192,768]{1,0:T(8,128)(2,1)}, bf16[192,768]{1,0:T(8,128)(2,1)}, u32[]{:S(2)}, u32[]{:S(2)}) collective-permute-start(bf16[192,768]{1,0:T(8,128)(2,1)} %collective-permute-done.t1), channel_id=1, source_target_pairs={{0,12},{1,13},{2,14},{3,15},{4,0},{5,1},{6,2},{7,3},{8,4},{9,5},{1... | collective-permute-start | bytes 884744 | tf_op jit(solution)/shard_map/ppermute | solution.py:20
  42.1 19.8 %collective-permute-start.6 = (bf16[192,768]{1,0:T(8,128)(2,1)}, bf16[192,768]{1,0:T(8,128)(2,1)}, u32[]{:S(2)}, u32[]{:S(2)}) collective-permute-start(bf16[192,768]{1,0:T(8,128)(2,1)} %collective-permute-done.4.t1), channel_id=1, source_target_pairs={{0,1},{1,0},{2,3},{3,2},{4,5},{5,4},{6,7},{7,6},{8,9},{9,8},{10,11... | collective-permute-start | bytes 884744 | tf_op jit(solution)/shard_map/ppermute | solution.py:20
  56.6 17.1 %collective-permute-start.12 = (bf16[192,768]{1,0:T(8,128)(2,1)}, bf16[192,768]{1,0:T(8,128)(2,1)}, u32[]{:S(2)}, u32[]{:S(2)}) collective-permute-start(bf16[192,768]{1,0:T(8,128)(2,1)} %collective-permute-done.t1), channel_id=1, source_target_pairs={{0,8},{1,9},{2,10},{3,11},{4,12},{5,13},{6,14},{7,15},{8,0},{9,1},... | collective-permute-start | bytes 884744 | tf_op jit(solution)/shard_map/ppermute | solution.py:20
  58.1 16.0 %collective-permute-start.11 = (bf16[192,768]{1,0:T(8,128)(2,1)}, bf16[192,768]{1,0:T(8,128)(2,1)}, u32[]{:S(2)}, u32[]{:S(2)}) collective-permute-start(bf16[192,768]{1,0:T(8,128)(2,1)} %collective-permute-done.t1), channel_id=1, source_target_pairs={{0,4},{1,5},{2,6},{3,7},{4,8},{5,9},{6,10},{7,11},{8,12},{9,13},{1... | collective-permute-start | bytes 884744 | tf_op jit(solution)/shard_map/ppermute | solution.py:20
  58.2 16.4 %collective-permute-start.2 = (bf16[192,768]{1,0:T(8,128)(2,1)}, bf16[192,768]{1,0:T(8,128)(2,1)}, u32[]{:S(2)}, u32[]{:S(2)}) collective-permute-start(bf16[192,768]{1,0:T(8,128)(2,1)} %collective-permute-done.t1), channel_id=1, source_target_pairs={{0,1},{1,0},{2,3},{3,2},{4,5},{5,4},{6,7},{7,6},{8,9},{9,8},{10,11... | collective-permute-start | bytes 884744 | tf_op jit(solution)/shard_map/ppermute | solution.py:20
  61.3 25.1 %collective-permute-start.9 = (bf16[192,768]{1,0:T(8,128)(2,1)S(1)}, bf16[192,768]{1,0:T(8,128)(2,1)S(1)}, u32[]{:S(2)}, u32[]{:S(2)}) collective-permute-start(bf16[192,768]{1,0:T(8,128)(2,1)S(1)} %collective-permute-done.7.t0), channel_id=1, source_target_pairs={{0,1},{1,0},{2,3},{3,2},{4,5},{5,4},{6,7},{7,6},{8,9},{9,8},{10,11... | collective-permute-start | bytes 884744 | tf_op jit(solution)/shard_map/ppermute | solution.py:20
  61.9 24.5 %collective-permute-start.10 = (bf16[192,768]{1,0:T(8,128)(2,1)}, bf16[192,768]{1,0:T(8,128)(2,1)S(1)}, u32[]{:S(2)}, u32[]{:S(2)}) collective-permute-start(bf16[192,768]{1,0:T(8,128)(2,1)} %collective-permute-done.8.t1), channel_id=1, source_target_pairs={{0,1},{1,0},{2,3},{3,2},{4,5},{5,4},{6,7},{7,6},{8,9},{9,8},{10,11... | collective-permute-start | bytes 884744 | tf_op jit(solution)/shard_map/ppermute | solution.py:20
  73.7 24.2 %collective-permute-start.14 = (bf16[192,768]{1,0:T(8,128)(2,1)}, bf16[192,768]{1,0:T(8,128)(2,1)S(1)}, u32[]{:S(2)}, u32[]{:S(2)}) collective-permute-start(bf16[192,768]{1,0:T(8,128)(2,1)} %collective-permute-done.12.t1), channel_id=1, source_target_pairs={{0,1},{1,0},{2,3},{3,2},{4,5},{5,4},{6,7},{7,6},{8,9},{9,8},{10,11... | collective-permute-start | bytes 884744 | tf_op jit(solution)/shard_map/ppermute | solution.py:20
  74.2 23.7 %collective-permute-start.13 = (bf16[192,768]{1,0:T(8,128)(2,1)}, bf16[192,768]{1,0:T(8,128)(2,1)S(1)}, u32[]{:S(2)}, u32[]{:S(2)}) collective-permute-start(bf16[192,768]{1,0:T(8,128)(2,1)} %collective-permute-done.11.t0), channel_id=1, source_target_pairs={{0,1},{1,0},{2,3},{3,2},{4,5},{5,4},{6,7},{7,6},{8,9},{9,8},{10,11... | collective-permute-start | bytes 884744 | tf_op jit(solution)/shard_map/ppermute | solution.py:20
  126.3 34.7 %all-to-all-start.4 = ((bf16[128,3,768]{2,1,0:T(4,128)(2,1)}), bf16[128,3,768]{2,1,0:T(4,128)(2,1)}, u32[]{:S(2)}, u32[]{:S(2)}) async-start(bf16[128,3,768]{2,1,0:T(4,128)(2,1)} %reshape.153), calls=%async_computation.4 | async-start | bytes 1572864 | tf_op jit(solution)/shard_map/all_to_all | solution.py:334
  142.4 60.6 %collective-permute-start.26 = (f32[384,768]{1,0:T(8,128)}, f32[384,768]{1,0:T(8,128)}, u32[]{:S(2)}, u32[]{:S(2)}) collective-permute-start(f32[384,768]{1,0:T(8,128)} %get-tuple-element.43), channel_id=1, source_target_pairs={{0,1},{1,0},{2,3},{3,2},{4,5},{5,4},{6,7},{7,6},{8,9},{9,8},{10,11... | collective-permute-start | bytes 3538952 | tf_op jit(solution)/shard_map/ppermute | solution.py:20
  161.0 56.5 %all-to-all-start.3 = ((bf16[8,192,768]{2,1,0:T(8,128)(2,1)}), bf16[8,192,768]{2,1,0:T(8,128)(2,1)}, u32[]{:S(2)}, u32[]{:S(2)}) async-start(bf16[8,192,768]{2,1,0:T(8,128)(2,1)} %bitcast.18), calls=%async_computation.3 | async-start | bytes 4718592 | tf_op jit(solution)/shard_map/all_to_all | solution.py:301
  185.2 22.2 %collective-permute-start.23 = (f32[384,768]{1,0:T(8,128)}, f32[384,768]{1,0:T(8,128)}, u32[]{:S(2)}, u32[]{:S(2)}) collective-permute-start(f32[384,768]{1,0:T(8,128)} %get-tuple-element.41), channel_id=1, source_target_pairs={{0,1},{1,0},{2,3},{3,2},{4,5},{5,4},{6,7},{7,6},{8,9},{9,8},{10,11... | collective-permute-start | bytes 3538952 | tf_op jit(solution)/shard_map/ppermute | solution.py:20
  193.1 19.7 %collective-permute-start.19 = (f32[384,768]{1,0:T(8,128)}, f32[384,768]{1,0:T(8,128)}, u32[]{:S(2)}, u32[]{:S(2)}) collective-permute-start(f32[384,768]{1,0:T(8,128)} %get-tuple-element.37), channel_id=1, source_target_pairs={{0,1},{1,0},{2,3},{3,2},{4,5},{5,4},{6,7},{7,6},{8,9},{9,8},{10,11... | collective-permute-start | bytes 3538952 | tf_op jit(solution)/shard_map/ppermute | solution.py:20
  200.3 15.7 %collective-permute-start.20 = (f32[384,768]{1,0:T(8,128)}, f32[384,768]{1,0:T(8,128)}, u32[]{:S(2)}, u32[]{:S(2)}) collective-permute-start(f32[384,768]{1,0:T(8,128)} %get-tuple-element.39), channel_id=1, source_target_pairs={{0,1},{1,0},{2,3},{3,2},{4,5},{5,4},{6,7},{7,6},{8,9},{9,8},{10,11... | collective-permute-start | bytes 3538952 | tf_op jit(solution)/shard_map/ppermute | solution.py:20
  205.7 16.4 %collective-permute-start.27 = (bf16[192,768]{1,0:T(8,128)(2,1)}, bf16[192,768]{1,0:T(8,128)(2,1)}, u32[]{:S(2)}, u32[]{:S(2)}) collective-permute-start(bf16[192,768]{1,0:T(8,128)(2,1)} %get-tuple-element.55), channel_id=1, source_target_pairs={{0,12},{1,13},{2,14},{3,15},{4,0},{5,1},{6,2},{7,3},{8,4},{9,5},{1... | collective-permute-start | bytes 884744 | tf_op jit(solution)/shard_map/ppermute | solution.py:20
  207.0 15.2 %collective-permute-start.28 = (bf16[192,768]{1,0:T(8,128)(2,1)}, bf16[192,768]{1,0:T(8,128)(2,1)}, u32[]{:S(2)}, u32[]{:S(2)}) collective-permute-start(bf16[192,768]{1,0:T(8,128)(2,1)} %get-tuple-element.56), channel_id=1, source_target_pairs={{0,8},{1,9},{2,10},{3,11},{4,12},{5,13},{6,14},{7,15},{8,0},{9,1},... | collective-permute-start | bytes 884744 | tf_op jit(solution)/shard_map/ppermute | solution.py:20
  209.7 33.9 %collective-permute-start.24 = (bf16[192,768]{1,0:T(8,128)(2,1)}, bf16[192,768]{1,0:T(8,128)(2,1)S(1)}, u32[]{:S(2)}, u32[]{:S(2)}) collective-permute-start(bf16[192,768]{1,0:T(8,128)(2,1)} %get-tuple-element.53), channel_id=1, source_target_pairs={{0,8},{1,9},{2,10},{3,11},{4,12},{5,13},{6,14},{7,15},{8,0},{9,1},... | collective-permute-start | bytes 884744 | tf_op jit(solution)/shard_map/ppermute | solution.py:20
  212.7 17.8 %collective-permute-start.25 = (bf16[192,768]{1,0:T(8,128)(2,1)}, bf16[192,768]{1,0:T(8,128)(2,1)}, u32[]{:S(2)}, u32[]{:S(2)}) collective-permute-start(bf16[192,768]{1,0:T(8,128)(2,1)} %get-tuple-element.54), channel_id=1, source_target_pairs={{0,4},{1,5},{2,6},{3,7},{4,8},{5,9},{6,10},{7,11},{8,12},{9,13},{1... | collective-permute-start | bytes 884744 | tf_op jit(solution)/shard_map/ppermute | solution.py:20
  220.9 18.1 %collective-permute-start.15 = (s16[192,768]{1,0:T(8,128)(2,1)S(1)}, s16[192,768]{1,0:T(8,128)(2,1)S(1)}, u32[]{:S(2)}, u32[]{:S(2)}) collective-permute-start(s16[192,768]{1,0:T(8,128)(2,1)S(1)} %get-tuple-element.50), channel_id=1, source_target_pairs={{0,16},{16,0},{32,48},{48,32},{64,80},{80,64},{96,112},{112,96},{1... | collective-permute-start | bytes 884744 | tf_op jit(solution)/shard_map/ppermute | solution.py:24
  231.8 17.4 %collective-permute-start.29 = (f32[192,768]{1,0:T(8,128)S(1)}, f32[192,768]{1,0:T(8,128)S(1)}, u32[]{:S(2)}, u32[]{:S(2)}) collective-permute-start(f32[192,768]{1,0:T(8,128)S(1)} %fusion.3), channel_id=1, source_target_pairs={{0,2},{1,3},{2,0},{3,1},{4,6},{5,7},{6,4},{7,5},{8,10},{9,11},{10,... | collective-permute-start | bytes 1769480 | tf_op jit(solution)/shard_map/ppermute | solution.py:20
  239.0 27.9 %collective-permute-start.16 = (s16[2,192,768]{2,1,0:T(8,128)(2,1)S(1)}, s16[2,192,768]{2,1,0:T(8,128)(2,1)S(1)}, u32[]{:S(2)}, u32[]{:S(2)}) collective-permute-start(s16[2,192,768]{2,1,0:T(8,128)(2,1)S(1)} %pad_add_fusion), channel_id=1, source_target_pairs={{0,96},{16,112},{32,0},{48,16},{64,32},{80,48},{96,64},{112,80},{1... | collective-permute-start | bytes 1769480 | tf_op jit(solution)/shard_map/ppermute | solution.py:24
  250.1 30.6 %collective-permute-start.18 = (s16[2,192,768]{2,1,0:T(8,128)(2,1)S(1)}, s16[2,192,768]{2,1,0:T(8,128)(2,1)S(1)}, u32[]{:S(2)}, u32[]{:S(2)}) collective-permute-start(s16[2,192,768]{2,1,0:T(8,128)(2,1)S(1)} %pad_add_fusion), channel_id=1, source_target_pairs={{0,32},{16,48},{32,64},{48,80},{64,96},{80,112},{96,0},{112,16},{1... | collective-permute-start | bytes 1769480 | tf_op jit(solution)/shard_map/ppermute | solution.py:24
  252.1 28.4 %collective-permute-start.17 = (s16[2,192,768]{2,1,0:T(8,128)(2,1)S(1)}, s16[2,192,768]{2,1,0:T(8,128)(2,1)S(1)}, u32[]{:S(2)}, u32[]{:S(2)}) collective-permute-start(s16[2,192,768]{2,1,0:T(8,128)(2,1)S(1)} %pad_add_fusion), channel_id=1, source_target_pairs={{0,64},{16,80},{32,96},{48,112},{64,0},{80,16},{96,32},{112,48},{1... | collective-permute-start | bytes 1769480 | tf_op jit(solution)/shard_map/ppermute | solution.py:24
  (43 other events, 459.4 us)
